TPU v7x, 32 devices: a whole 2x2x4 slice. The times are simulated.
32 devices in a mesh: job: 2 (over x), tm: 2 (over core), rows: 8 (over z, y).
Axes of the slice: x: 2, y: 2, z: 4, core: 2. Of those that a mesh axis runs over, the one named last changes fastest.
Arguments:
- prior: bfloat16 [2, 524288, 64], P('tm', ('job', 'rows')), parts along dimension 1, may hold values from -80 to 80
- snapshots: bfloat16 [2, 524288, 256], P('tm', ('job', 'rows')), parts along dimension 1, may hold values from -60 to 60
Outputs:
- merged: bfloat16 [524288, 64], P(('job', 'rows'), 'tm'), parts along dimension 0
There are 2 independent parts, one for each index of `job`. A program takes and returns all parts, laid end to end along the dimension named above; each array names one. Nothing has to cross between parts.
All inputs are finite; a program needn't handle non-finite values.
Results may differ from a plain program's by a relative error of at most 0.011.
Values may be sent and summed in bfloat16 or wider, within the bound.
A program may use at most 128 MiB of HBM per device.

v0:
```python
import jax
import jax.numpy as jnp
from jax import lax
from jax.sharding import PartitionSpec as P

STEPS = 4
ITERS = 2


def partner(block, axis, bit):
    count = lax.axis_size(axis)
    route = []
    for low in range(count):
        high = low | 1 << bit
        if high != low and high < count:
            route += [(low, high), (high, low)]
    return lax.ppermute(block, axis, route)


def basis_of(gram, keep):
    order = gram.shape[0]
    basis = jnp.eye(order, keep, dtype=jnp.float32)
    for turn in range(ITERS):
        image = jnp.dot(gram, basis, precision=lax.Precision.HIGHEST)
        inner = jnp.dot(image.T, image, precision=lax.Precision.HIGHEST)
        lower = jnp.linalg.cholesky(inner)
        basis = jax.scipy.linalg.solve_triangular(lower, image.T, lower=True).T
    return basis


def project(joined, basis):
    return jnp.dot(
        joined, basis, precision=lax.Precision.HIGHEST, preferred_element_type=jnp.float32
    )


def inner_rows(left, right):
    return jnp.dot(
        left.T, right, precision=lax.Precision.HIGHEST, preferred_element_type=jnp.float32
    )


def shards(prior, snapshots):
    start_modes = prior[0]
    frames = snapshots[0]
    keep = start_modes.shape[1]
    fresh_cols = frames.shape[1] // STEPS
    whole = jnp.concatenate([start_modes, frames], axis=1)
    total = lax.psum(jnp.dot(whole.T, whole, preferred_element_type=jnp.float32), "rows")
    width = whole.shape[1]
    weights = jnp.eye(width, keep, dtype=jnp.float32)
    for step in range(STEPS):
        picker = jnp.eye(width, fresh_cols, k=-(keep + step * fresh_cols), dtype=jnp.float32)
        coeffs = jnp.concatenate([weights, picker], axis=1)
        applied = jnp.dot(total, coeffs, precision=lax.Precision.HIGHEST)
        gram = jnp.dot(coeffs.T, applied, precision=lax.Precision.HIGHEST)
        weights = jnp.dot(coeffs, basis_of(gram, keep), precision=lax.Precision.HIGHEST)
    modes = project(whole, weights)
    index = lax.axis_index("tm")
    half_keep = keep // 2
    other = partner(modes.astype(jnp.bfloat16), "tm", 0).astype(modes.dtype)
    first = jnp.where(index == 0, modes, other)
    second = jnp.where(index == 0, other, modes)
    joined = jnp.concatenate([first, second], axis=1)
    gram = lax.psum(inner_rows(joined, joined).astype(jnp.bfloat16), "rows").astype(jnp.float32)
    full_merge = project(joined, basis_of(gram, keep)).astype(jnp.bfloat16)
    merged = lax.dynamic_slice_in_dim(full_merge, index * half_keep, half_keep, 1)
    return merged


def solution(mesh):
    in_specs = (P("tm", ("job", "rows"), None), P("tm", ("job", "rows"), None))
    out_specs = P(("job", "rows"), "tm")
    return jax.shard_map(shards, mesh=mesh, in_specs=in_specs, out_specs=out_specs, check_vma=False)
```

profile of v0, /device:TPU:0, one launch (start us, length us, event | category | flops | bytes accessed | tf_op | source)
XLA Modules:
  0.0 384.0 jit_solution(9080420248376913407)
XLA Ops:
  6.5 8.5 %copy.3 = bf16[1,32768,64]{2,1,0:T(8,128)(2,1)} copy(bf16[1,32768,64]{1,2,0:T(8,128)(2,1)} %param.5) | data formatting | bytes 8388608 | tf_op args[0]
  15.0 30.9 %fusion.1 = f32[320,320]{1,0:T(8,128)} fusion(bf16[32768,256]{1,0:T(8,128)(2,1)} %bitcast.173, bf16[32768,64]{1,0:T(8,128)(2,1)} %bitcast.171), kind=kOutput, calls=%fused_computation.3 | convolution fusion | flops 6752829440 | bytes 21381120 | tf_op jit(solution)/shard_map/dot_general | solution.py:49
  46.2 75.3 %all-reduce.2.cloned.1.call-done = f32[320,320]{1,0:T(8,128)} async-done(((f32[320,320]{1,0:T(8,128)}), f32[320,320]{1,0:T(8,128)}) %all-reduce.2.cloned.1.call-update) | async-done | bytes 409616 | tf_op jit(solution)/shard_map/psum | solution.py:49
  121.5 1.4 fusion.88
  122.9 0.4 fusion.87
  123.9 5.8 %cholesky.164 = f32[64,64]{1,0:T(8,128)S(1)} custom-call(f32[64,64]{1,0:T(8,128)S(1)} %fusion.71), custom_call_target="Cholesky" | custom-call | tf_op jit(solution)/shard_map/jit(cholesky)/cholesky | solution.py:26
  129.8 0.6 compare_reduce_fusion.9
  130.4 0.7 fusion.22
  131.1 4.9 %custom-call.14 = f32[1,64,64]{1,2,0:T(8,128)S(1)} custom-call(f32[1,64,64]{2,1,0:T(8,128)S(1)} %fusion.22), custom_call_target="InvertDiagBlocksLowerTriangular" | custom-call | tf_op jit(solution)/shard_map/jit(_solve_triangular)/triangular_solve | solution.py:27
  136.0 0.3 fusion.68
  136.8 5.8 %cholesky.175 = f32[64,64]{1,0:T(8,128)S(1)} custom-call(f32[64,64]{1,0:T(8,128)S(1)} %fusion.67), custom_call_target="Cholesky" | custom-call | tf_op jit(solution)/shard_map/jit(cholesky)/cholesky | solution.py:26
  142.7 0.6 compare_reduce_fusion.8
  143.3 0.7 fusion.23
  144.0 4.9 %custom-call.15 = f32[1,64,64]{1,2,0:T(8,128)S(1)} custom-call(f32[1,64,64]{2,1,0:T(8,128)S(1)} %fusion.23), custom_call_target="InvertDiagBlocksLowerTriangular" | custom-call | tf_op jit(solution)/shard_map/jit(_solve_triangular)/triangular_solve | solution.py:27
  148.9 0.3 fusion.64
  149.1 0.3 fusion.89
  149.4 1.6 fusion.13
  151.0 0.3 fusion.12
  151.9 5.8 %cholesky.186 = f32[64,64]{1,0:T(8,128)S(1)} custom-call(f32[64,64]{1,0:T(8,128)S(1)} %fusion.63), custom_call_target="Cholesky" | custom-call | tf_op jit(solution)/shard_map/jit(cholesky)/cholesky | solution.py:26
  157.8 0.6 compare_reduce_fusion.7
  158.4 0.7 fusion.24
  159.1 4.9 %custom-call.16 = f32[1,64,64]{1,2,0:T(8,128)S(1)} custom-call(f32[1,64,64]{2,1,0:T(8,128)S(1)} %fusion.24), custom_call_target="InvertDiagBlocksLowerTriangular" | custom-call | tf_op jit(solution)/shard_map/jit(_solve_triangular)/triangular_solve | solution.py:27
  164.7 5.8 %cholesky.197 = f32[64,64]{1,0:T(8,128)S(1)} custom-call(f32[64,64]{1,0:T(8,128)S(1)} %fusion.59), custom_call_target="Cholesky" | custom-call | tf_op jit(solution)/shard_map/jit(cholesky)/cholesky | solution.py:26
  170.6 0.6 compare_reduce_fusion.6
  171.3 0.7 fusion.25
  171.9 4.9 %custom-call.17 = f32[1,64,64]{1,2,0:T(8,128)S(1)} custom-call(f32[1,64,64]{2,1,0:T(8,128)S(1)} %fusion.25), custom_call_target="InvertDiagBlocksLowerTriangular" | custom-call | tf_op jit(solution)/shard_map/jit(_solve_triangular)/triangular_solve | solution.py:27
  177.1 0.3 fusion.11
  177.4 1.6 fusion.10
  179.0 0.3 fusion.9
  179.8 6.0 %cholesky.208 = f32[64,64]{1,0:T(8,128)S(1)} custom-call(f32[64,64]{1,0:T(8,128)S(1)} %fusion.55), custom_call_target="Cholesky" | custom-call | tf_op jit(solution)/shard_map/jit(cholesky)/cholesky | solution.py:26
  185.9 0.6 compare_reduce_fusion.5
  186.5 0.7 fusion.26
  187.2 4.9 %custom-call.18 = f32[1,64,64]{1,2,0:T(8,128)S(1)} custom-call(f32[1,64,64]{2,1,0:T(8,128)S(1)} %fusion.26), custom_call_target="InvertDiagBlocksLowerTriangular" | custom-call | tf_op jit(solution)/shard_map/jit(_solve_triangular)/triangular_solve | solution.py:27
  192.9 5.8 %cholesky.219 = f32[64,64]{1,0:T(8,128)S(1)} custom-call(f32[64,64]{1,0:T(8,128)S(1)} %fusion.51), custom_call_target="Cholesky" | custom-call | tf_op jit(solution)/shard_map/jit(cholesky)/cholesky | solution.py:26
  198.8 0.6 compare_reduce_fusion.4
  199.4 0.7 fusion.27
  200.1 4.9 %custom-call.19 = f32[1,64,64]{1,2,0:T(8,128)S(1)} custom-call(f32[1,64,64]{2,1,0:T(8,128)S(1)} %fusion.27), custom_call_target="InvertDiagBlocksLowerTriangular" | custom-call | tf_op jit(solution)/shard_map/jit(_solve_triangular)/triangular_solve | solution.py:27
  205.2 0.3 fusion.8
  205.5 1.6 fusion.7
  207.1 0.3 fusion.6
  208.0 5.8 %cholesky.230 = f32[64,64]{1,0:T(8,128)S(1)} custom-call(f32[64,64]{1,0:T(8,128)S(1)} %fusion.47), custom_call_target="Cholesky" | custom-call | tf_op jit(solution)/shard_map/jit(cholesky)/cholesky | solution.py:26
  213.8 0.6 compare_reduce_fusion.3
  214.5 0.7 fusion.28
  215.1 4.9 %custom-call.20 = f32[1,64,64]{1,2,0:T(8,128)S(1)} custom-call(f32[1,64,64]{2,1,0:T(8,128)S(1)} %fusion.28), custom_call_target="InvertDiagBlocksLowerTriangular" | custom-call | tf_op jit(solution)/shard_map/jit(_solve_triangular)/triangular_solve | solution.py:27
  220.8 5.8 %cholesky.241 = f32[64,64]{1,0:T(8,128)S(1)} custom-call(f32[64,64]{1,0:T(8,128)S(1)} %fusion.43), custom_call_target="Cholesky" | custom-call | tf_op jit(solution)/shard_map/jit(cholesky)/cholesky | solution.py:26
  226.7 0.6 compare_reduce_fusion.2
  227.4 0.7 fusion.29
  228.0 4.9 %custom-call.21 = f32[1,64,64]{1,2,0:T(8,128)S(1)} custom-call(f32[1,64,64]{2,1,0:T(8,128)S(1)} %fusion.29), custom_call_target="InvertDiagBlocksLowerTriangular" | custom-call | tf_op jit(solution)/shard_map/jit(_solve_triangular)/triangular_solve | solution.py:27
  233.2 0.5 fusion.5
  233.7 29.1 %fusion.90 = (bf16[32768,64]{0,1:T(8,128)(2,1)}, f32[32768,64]{0,1:T(8,128)}) fusion(f32[320,64]{1,0:T(8,128)S(1)} %fusion.5, bf16[32768,256]{1,0:T(8,128)(2,1)} %bitcast.174, bf16[32768,64]{1,0:T(8,128)(2,1)} %bitcast.172), kind=kOutput, calls=%fused_computation.150 | convolution fusion | flops 8097103872 | bytes 33636352 | tf_op jit(solution)/shard_map/dot_general | solution.py:32
  262.7 7.5 %collective-permute-done = bf16[32768,64]{0,1:T(8,128)(2,1)} collective-permute-done((bf16[32768,64]{0,1:T(8,128)(2,1)}, bf16[32768,64]{0,1:T(8,128)(2,1)}, u32[]{:S(2)}, u32[]{:S(2)}) %collective-permute-start) | collective-permute-done | bytes 4194336 | tf_op jit(solution)/shard_map/ppermute | solution.py:17
  270.2 12.1 %convert_select_fusion.1 = (f32[32768,64]{0,1:T(8,128)}, f32[32768,64]{0,1:T(8,128)}) fusion(f32[32768,64]{0,1:T(8,128)} %get-tuple-element.10, bf16[32768,64]{0,1:T(8,128)(2,1)} %collective-permute-done, pred[]{:T(512)S(6)} %eq.34), kind=kLoop, calls=%fused_computation.7 | loop fusion | flops 6291456 | bytes 29360128 | tf_op jit(solution)/shard_map/jit(_where)/select_n | solution.py:62
  282.3 18.3 %fusion.4 = bf16[128,128]{1,0:T(8,128)(2,1)S(1)} fusion(f32[32768,64]{0,1:T(8,128)} %get-tuple-element.8, f32[32768,64]{0,1:T(8,128)} %get-tuple-element.6), kind=kOutput, calls=%fused_computation.9 | convolution fusion | flops 6446661632 | bytes 16809984 | tf_op jit(solution)/shard_map/dot_general | solution.py:38
  300.6 35.4 %psum.15 = bf16[128,128]{1,0:T(8,128)(2,1)S(1)} all-reduce(bf16[128,128]{1,0:T(8,128)(2,1)S(1)} %fusion.4), channel_id=1, replica_groups=mesh['job'=2,'tm'=2,'rows'=8] {'rows'}, use_global_device_ids=true, to_apply=%region_3.6 | all-reduce | flops 16384 | bytes 65536 | tf_op jit(solution)/shard_map/psum | solution.py:65
  336.5 5.8 %cholesky.252 = f32[64,64]{1,0:T(8,128)S(1)} custom-call(f32[64,64]{1,0:T(8,128)S(1)} %fusion.39), custom_call_target="Cholesky" | custom-call | tf_op jit(solution)/shard_map/jit(cholesky)/cholesky | solution.py:26
  342.4 0.6 compare_reduce_fusion.1
  343.1 0.7 fusion.30
  343.7 4.9 %custom-call.22 = f32[1,64,64]{1,2,0:T(8,128)S(1)} custom-call(f32[1,64,64]{2,1,0:T(8,128)S(1)} %fusion.30), custom_call_target="InvertDiagBlocksLowerTriangular" | custom-call | tf_op jit(solution)/shard_map/jit(_solve_triangular)/triangular_solve | solution.py:27
  349.4 5.8 %cholesky.263 = f32[64,64]{1,0:T(8,128)S(1)} custom-call(f32[64,64]{1,0:T(8,128)S(1)} %fusion.35), custom_call_target="Cholesky" | custom-call | tf_op jit(solution)/shard_map/jit(cholesky)/cholesky | solution.py:26
  355.3 0.6 compare_reduce_fusion
  355.9 0.7 fusion.31
  356.6 4.9 %custom-call.23 = f32[1,64,64]{1,2,0:T(8,128)S(1)} custom-call(f32[1,64,64]{2,1,0:T(8,128)S(1)} %fusion.31), custom_call_target="InvertDiagBlocksLowerTriangular" | custom-call | tf_op jit(solution)/shard_map/jit(_solve_triangular)/triangular_solve | solution.py:27
  361.7 13.8 %fusion.2 = bf16[32768,64]{0,1:T(8,128)(2,1)S(1)} fusion(f32[64,128]{1,0:T(8,128)S(1)} %fusion.32, f32[32768,64]{0,1:T(8,128)} %get-tuple-element.8, f32[32768,64]{0,1:T(8,128)} %get-tuple-element.6), kind=kOutput, calls=%fused_computation.4 | convolution fusion | flops 3225419776 | bytes 21004288 | tf_op jit(solution)/shard_map/dot_general | solution.py:32
  375.5 1.5 dynamic-slice_convert_fusion
  (69 shorter events, 7.4 us)
Async XLA Ops:
  6.5 115.0 %all-reduce.2.cloned.1.call-start = ((), (), s32[]{:S(2)}) async-start(), calls=%async_computation | async-start | bytes 983040 | tf_op jit(solution)/shard_map/psum | solution.py:49
  262.7 7.5 %collective-permute-start = (bf16[32768,64]{0,1:T(8,128)(2,1)}, bf16[32768,64]{0,1:T(8,128)(2,1)}, u32[]{:S(2)}, u32[]{:S(2)}) collective-permute-start(bf16[32768,64]{0,1:T(8,128)(2,1)} %get-tuple-element.9), channel_id=1, source_target_pairs={{0,8},{8,0},{1,9},{9,1},{2,10},{10,2},{3,11},{11,3},{4,12},{12,4},... | collective-permute-start | bytes 12582920 | tf_op jit(solution)/shard_map/ppermute | solution.py:17
Sparse Core Ops, SparseCore 0:
  46.1 75.3 all-reduce.1
where the time goes:
time: 389 us; the launch traced here: 384 us
  other arithmetic  133 us (34%)
  matrix products  108 us (28%)
  waiting for transfers between devices  82.9 us (21%)
  blocking collectives  35.4 us (9%)
  between operations  14.2 us (4%)
  local copies, waits for them, and re-layouts  10.7 us (3%)
    psum x1, waiting for transfers between devices, shards(): lax.psum(jnp.dot(whole.T, whole, preferred_element_type=jnp.float32), 'ro...  75.3 us
    another operation x30, other arithmetic, basis_of(): lower = jnp.linalg.cholesky(inner)  65.4 us
    another operation x20, other arithmetic, basis_of(): basis = jax.scipy.linalg.solve_triangular(lower, image.T, lower=True).T  55.5 us
    dot_general x2, matrix products, project(): jnp.dot(joined, basis, precision=lax.Precision.HIGHEST, preferred_element...  42.9 us
    psum x1, blocking collectives, shards(): lax.psum(inner_rows(joined, joined).astype(jnp.bfloat16), 'rows')  35.4 us
    dot_general x1, matrix products, shards(): jnp.dot(whole.T, whole, preferred_element_type=jnp.float32)  30.9 us
    dot_general x1, matrix products, inner_rows(): jnp.dot(left.T, right, precision=lax.Precision.HIGHEST, preferred_element...  18.3 us
    select_n x1, other arithmetic, shards(): first = jnp.where(index == 0, modes, other)  12.1 us
  transfers between devices with their start and end apart: 2, of which 2 were waited for; matrix products, arithmetic and copies ran while one was open for 0% of the time, Pallas kernels for 0%

commit v1 on v0

--- a/solution.py
+++ b/solution.py
@@ -62,7 +62,9 @@
     first = jnp.where(index == 0, modes, other)
     second = jnp.where(index == 0, other, modes)
     joined = jnp.concatenate([first, second], axis=1)
-    gram = lax.psum(inner_rows(joined, joined).astype(jnp.bfloat16), "rows").astype(jnp.float32)
+    gram = jnp.sum(
+        lax.all_gather(inner_rows(joined, joined).astype(jnp.bfloat16), "rows"), axis=0
+    ).astype(jnp.float32)
     full_merge = project(joined, basis_of(gram, keep)).astype(jnp.bfloat16)
     merged = lax.dynamic_slice_in_dim(full_merge, index * half_keep, half_keep, 1)
     return merged

time: 389 us -> 386 us (level)
  blocking collectives: 35.4 us -> 30.8 us
    psum x1 -> x0, blocking collectives: 35.4 us -> none  [shards(): lax.psum(inner_rows(joined, joined).astype(jnp.bfloat16), 'rows')]
    all_gather x0 -> x1, blocking collectives: none -> 30.8 us  [shards(): lax.all_gather(inner_rows(joined, joined).astype(jnp.bfloat16), 'rows')]
where the time goes in v1:
time: 386 us; the launch traced here: 380 us
  other arithmetic  133 us (34%)
  matrix products  108 us (28%)
  waiting for transfers between devices  82.8 us (21%)
  blocking collectives  30.8 us (8%)
  between operations  14.5 us (4%)
  local copies, waits for them, and re-layouts  10.7 us (3%)
    psum x1, waiting for transfers between devices, shards(): lax.psum(jnp.dot(whole.T, whole, preferred_element_type=jnp.float32), 'ro...  75.3 us
    another operation x30, other arithmetic, basis_of(): lower = jnp.linalg.cholesky(inner)  65.3 us
    another operation x20, other arithmetic, basis_of(): basis = jax.scipy.linalg.solve_triangular(lower, image.T, lower=True).T  55.5 us
    dot_general x2, matrix products, project(): jnp.dot(joined, basis, precision=lax.Precision.HIGHEST, preferred_element...  43 us
    dot_general x1, matrix products, shards(): jnp.dot(whole.T, whole, preferred_element_type=jnp.float32)  31.2 us
    all_gather x1, blocking collectives, shards(): lax.all_gather(inner_rows(joined, joined).astype(jnp.bfloat16), 'rows')  30.8 us
    dot_general x1, matrix products, inner_rows(): jnp.dot(left.T, right, precision=lax.Precision.HIGHEST, preferred_element...  18.6 us
    select_n x1, other arithmetic, shards(): first = jnp.where(index == 0, modes, other)  12.1 us
  transfers between devices with their start and end apart: 2, of which 2 were waited for; matrix products, arithmetic and copies ran while one was open for 0% of the time, Pallas kernels for 0%

profile of v1, /device:TPU:0, one launch (start us, length us, event | category | flops | bytes accessed | tf_op | source)
XLA Modules:
  0.0 380.3 jit_solution(17910566507054814284)
XLA Ops:
  6.5 8.5 %copy.3 = bf16[1,32768,64]{2,1,0:T(8,128)(2,1)} copy(bf16[1,32768,64]{1,2,0:T(8,128)(2,1)} %param.5) | data formatting | bytes 8388608 | tf_op args[0]
  15.0 31.2 %fusion.1 = f32[320,320]{1,0:T(8,128)} fusion(bf16[32768,256]{1,0:T(8,128)(2,1)} %bitcast.175, bf16[32768,64]{1,0:T(8,128)(2,1)} %bitcast.172), kind=kOutput, calls=%fused_computation.3 | convolution fusion | flops 6752829440 | bytes 21381120 | tf_op jit(solution)/shard_map/dot_general | solution.py:49
  46.5 75.3 %all-reduce.2.cloned.1.call-done = f32[320,320]{1,0:T(8,128)} async-done(((f32[320,320]{1,0:T(8,128)}), f32[320,320]{1,0:T(8,128)}) %all-reduce.2.cloned.1.call-update) | async-done | bytes 409616 | tf_op jit(solution)/shard_map/psum | solution.py:49
  121.8 1.4 fusion.88
  123.3 0.4 fusion.87
  124.2 5.8 %cholesky.164 = f32[64,64]{1,0:T(8,128)S(1)} custom-call(f32[64,64]{1,0:T(8,128)S(1)} %fusion.71), custom_call_target="Cholesky" | custom-call | tf_op jit(solution)/shard_map/jit(cholesky)/cholesky | solution.py:26
  130.1 0.6 compare_reduce_fusion.9
  130.8 0.7 fusion.22
  131.4 4.9 %custom-call.14 = f32[1,64,64]{1,2,0:T(8,128)S(1)} custom-call(f32[1,64,64]{2,1,0:T(8,128)S(1)} %fusion.22), custom_call_target="InvertDiagBlocksLowerTriangular" | custom-call | tf_op jit(solution)/shard_map/jit(_solve_triangular)/triangular_solve | solution.py:27
  136.3 0.3 fusion.68
  137.1 5.8 %cholesky.175 = f32[64,64]{1,0:T(8,128)S(1)} custom-call(f32[64,64]{1,0:T(8,128)S(1)} %fusion.67), custom_call_target="Cholesky" | custom-call | tf_op jit(solution)/shard_map/jit(cholesky)/cholesky | solution.py:26
  143.0 0.6 compare_reduce_fusion.8
  143.6 0.7 fusion.23
  144.3 4.9 %custom-call.15 = f32[1,64,64]{1,2,0:T(8,128)S(1)} custom-call(f32[1,64,64]{2,1,0:T(8,128)S(1)} %fusion.23), custom_call_target="InvertDiagBlocksLowerTriangular" | custom-call | tf_op jit(solution)/shard_map/jit(_solve_triangular)/triangular_solve | solution.py:27
  149.4 0.3 fusion.89
  149.7 1.6 fusion.13
  151.3 0.3 fusion.12
  152.2 5.8 %cholesky.186 = f32[64,64]{1,0:T(8,128)S(1)} custom-call(f32[64,64]{1,0:T(8,128)S(1)} %fusion.63), custom_call_target="Cholesky" | custom-call | tf_op jit(solution)/shard_map/jit(cholesky)/cholesky | solution.py:26
  158.1 0.6 compare_reduce_fusion.7
  158.7 0.7 fusion.24
  159.4 4.9 %custom-call.16 = f32[1,64,64]{1,2,0:T(8,128)S(1)} custom-call(f32[1,64,64]{2,1,0:T(8,128)S(1)} %fusion.24), custom_call_target="InvertDiagBlocksLowerTriangular" | custom-call | tf_op jit(solution)/shard_map/jit(_solve_triangular)/triangular_solve | solution.py:27
  165.1 5.8 %cholesky.197 = f32[64,64]{1,0:T(8,128)S(1)} custom-call(f32[64,64]{1,0:T(8,128)S(1)} %fusion.59), custom_call_target="Cholesky" | custom-call | tf_op jit(solution)/shard_map/jit(cholesky)/cholesky | solution.py:26
  170.9 0.6 compare_reduce_fusion.6
  171.6 0.7 fusion.25
  172.2 4.9 %custom-call.17 = f32[1,64,64]{1,2,0:T(8,128)S(1)} custom-call(f32[1,64,64]{2,1,0:T(8,128)S(1)} %fusion.25), custom_call_target="InvertDiagBlocksLowerTriangular" | custom-call | tf_op jit(solution)/shard_map/jit(_solve_triangular)/triangular_solve | solution.py:27
  177.4 0.3 fusion.11
  177.7 1.6 fusion.10
  179.3 0.3 fusion.9
  180.1 6.0 %cholesky.208 = f32[64,64]{1,0:T(8,128)S(1)} custom-call(f32[64,64]{1,0:T(8,128)S(1)} %fusion.55), custom_call_target="Cholesky" | custom-call | tf_op jit(solution)/shard_map/jit(cholesky)/cholesky | solution.py:26
  186.2 0.6 compare_reduce_fusion.5
  186.8 0.7 fusion.26
  187.5 4.9 %custom-call.18 = f32[1,64,64]{1,2,0:T(8,128)S(1)} custom-call(f32[1,64,64]{2,1,0:T(8,128)S(1)} %fusion.26), custom_call_target="InvertDiagBlocksLowerTriangular" | custom-call | tf_op jit(solution)/shard_map/jit(_solve_triangular)/triangular_solve | solution.py:27
  193.2 5.8 %cholesky.219 = f32[64,64]{1,0:T(8,128)S(1)} custom-call(f32[64,64]{1,0:T(8,128)S(1)} %fusion.51), custom_call_target="Cholesky" | custom-call | tf_op jit(solution)/shard_map/jit(cholesky)/cholesky | solution.py:26
  199.0 0.6 compare_reduce_fusion.4
  199.7 0.7 fusion.27
  200.3 4.9 %custom-call.19 = f32[1,64,64]{1,2,0:T(8,128)S(1)} custom-call(f32[1,64,64]{2,1,0:T(8,128)S(1)} %fusion.27), custom_call_target="InvertDiagBlocksLowerTriangular" | custom-call | tf_op jit(solution)/shard_map/jit(_solve_triangular)/triangular_solve | solution.py:27
  205.5 0.3 fusion.8
  205.8 1.6 fusion.7
  207.4 0.3 fusion.6
  208.2 5.8 %cholesky.230 = f32[64,64]{1,0:T(8,128)S(1)} custom-call(f32[64,64]{1,0:T(8,128)S(1)} %fusion.47), custom_call_target="Cholesky" | custom-call | tf_op jit(solution)/shard_map/jit(cholesky)/cholesky | solution.py:26
  214.1 0.6 compare_reduce_fusion.3
  214.8 0.7 fusion.28
  215.4 4.9 %custom-call.20 = f32[1,64,64]{1,2,0:T(8,128)S(1)} custom-call(f32[1,64,64]{2,1,0:T(8,128)S(1)} %fusion.28), custom_call_target="InvertDiagBlocksLowerTriangular" | custom-call | tf_op jit(solution)/shard_map/jit(_solve_triangular)/triangular_solve | solution.py:27
  221.1 5.8 %cholesky.241 = f32[64,64]{1,0:T(8,128)S(1)} custom-call(f32[64,64]{1,0:T(8,128)S(1)} %fusion.43), custom_call_target="Cholesky" | custom-call | tf_op jit(solution)/shard_map/jit(cholesky)/cholesky | solution.py:26
  227.0 0.6 compare_reduce_fusion.2
  227.6 0.7 fusion.29
  228.3 4.9 %custom-call.21 = f32[1,64,64]{1,2,0:T(8,128)S(1)} custom-call(f32[1,64,64]{2,1,0:T(8,128)S(1)} %fusion.29), custom_call_target="InvertDiagBlocksLowerTriangular" | custom-call | tf_op jit(solution)/shard_map/jit(_solve_triangular)/triangular_solve | solution.py:27
  233.5 0.5 fusion.5
  233.9 28.9 %fusion.90 = (bf16[32768,64]{0,1:T(8,128)(2,1)}, f32[32768,64]{0,1:T(8,128)}) fusion(f32[320,64]{1,0:T(8,128)S(1)} %fusion.5, bf16[32768,256]{1,0:T(8,128)(2,1)} %bitcast.176, bf16[32768,64]{1,0:T(8,128)(2,1)} %bitcast.173), kind=kOutput, calls=%fused_computation.150 | convolution fusion | flops 8097103872 | bytes 33636352 | tf_op jit(solution)/shard_map/dot_general | solution.py:32
  262.8 7.5 %collective-permute-done = bf16[32768,64]{0,1:T(8,128)(2,1)} collective-permute-done((bf16[32768,64]{0,1:T(8,128)(2,1)}, bf16[32768,64]{0,1:T(8,128)(2,1)}, u32[]{:S(2)}, u32[]{:S(2)}) %collective-permute-start) | collective-permute-done | bytes 4194336 | tf_op jit(solution)/shard_map/ppermute | solution.py:17
  270.3 12.1 %convert_select_fusion.1 = (f32[32768,64]{0,1:T(8,128)}, f32[32768,64]{0,1:T(8,128)}) fusion(f32[32768,64]{0,1:T(8,128)} %get-tuple-element.10, bf16[32768,64]{0,1:T(8,128)(2,1)} %collective-permute-done, pred[]{:T(512)S(6)} %eq.34), kind=kLoop, calls=%fused_computation.7 | loop fusion | flops 6291456 | bytes 29360128 | tf_op jit(solution)/shard_map/jit(_where)/select_n | solution.py:62
  282.4 18.6 %fusion.4 = bf16[128,128]{1,0:T(8,128)(2,1)S(1)} fusion(f32[32768,64]{0,1:T(8,128)} %get-tuple-element.8, f32[32768,64]{0,1:T(8,128)} %get-tuple-element.6), kind=kOutput, calls=%fused_computation.9 | convolution fusion | flops 6446661632 | bytes 16809984 | tf_op jit(solution)/shard_map/dot_general | solution.py:38
  301.0 30.8 %all-gather = bf16[1024,128]{1,0:T(8,128)(2,1)S(1)} all-gather(bf16[128,128]{1,0:T(8,128)(2,1)S(1)} %fusion.4), channel_id=2, replica_groups=mesh['job'=2,'tm'=2,'rows'=8] {'rows'}, dimensions={0}, use_global_device_ids=true | all-gather | bytes 294912 | tf_op jit(solution)/shard_map/all_gather | solution.py:66
  332.3 5.8 %cholesky.252 = f32[64,64]{1,0:T(8,128)S(1)} custom-call(f32[64,64]{1,0:T(8,128)S(1)} %fusion.39), custom_call_target="Cholesky" | custom-call | tf_op jit(solution)/shard_map/jit(cholesky)/cholesky | solution.py:26
  338.1 0.6 compare_reduce_fusion.1
  338.8 0.7 fusion.30
  339.4 4.9 %custom-call.22 = f32[1,64,64]{1,2,0:T(8,128)S(1)} custom-call(f32[1,64,64]{2,1,0:T(8,128)S(1)} %fusion.30), custom_call_target="InvertDiagBlocksLowerTriangular" | custom-call | tf_op jit(solution)/shard_map/jit(_solve_triangular)/triangular_solve | solution.py:27
  345.1 5.8 %cholesky.263 = f32[64,64]{1,0:T(8,128)S(1)} custom-call(f32[64,64]{1,0:T(8,128)S(1)} %fusion.35), custom_call_target="Cholesky" | custom-call | tf_op jit(solution)/shard_map/jit(cholesky)/cholesky | solution.py:26
  351.0 0.6 compare_reduce_fusion
  351.6 0.7 fusion.31
  352.3 4.9 %custom-call.23 = f32[1,64,64]{1,2,0:T(8,128)S(1)} custom-call(f32[1,64,64]{2,1,0:T(8,128)S(1)} %fusion.31), custom_call_target="InvertDiagBlocksLowerTriangular" | custom-call | tf_op jit(solution)/shard_map/jit(_solve_triangular)/triangular_solve | solution.py:27
  357.2 0.3 fusion.32
  357.4 14.1 %fusion.2 = bf16[32768,64]{0,1:T(8,128)(2,1)S(1)} fusion(f32[64,128]{1,0:T(8,128)S(1)} %fusion.32, f32[32768,64]{0,1:T(8,128)} %get-tuple-element.8, f32[32768,64]{0,1:T(8,128)} %get-tuple-element.6), kind=kOutput, calls=%fused_computation.4 | convolution fusion | flops 3225419776 | bytes 21004288 | tf_op jit(solution)/shard_map/dot_general | solution.py:32
  371.5 1.5 dynamic-slice_convert_fusion
  (70 shorter events, 7.5 us)
Async XLA Ops:
  6.5 115.3 %all-reduce.2.cloned.1.call-start = ((), (), s32[]{:S(2)}) async-start(), calls=%async_computation | async-start | bytes 983040 | tf_op jit(solution)/shard_map/psum | solution.py:49
  262.8 7.5 %collective-permute-start = (bf16[32768,64]{0,1:T(8,128)(2,1)}, bf16[32768,64]{0,1:T(8,128)(2,1)}, u32[]{:S(2)}, u32[]{:S(2)}) collective-permute-start(bf16[32768,64]{0,1:T(8,128)(2,1)} %get-tuple-element.9), channel_id=1, source_target_pairs={{0,8},{8,0},{1,9},{9,1},{2,10},{10,2},{3,11},{11,3},{4,12},{12,4},... | collective-permute-start | bytes 12582920 | tf_op jit(solution)/shard_map/ppermute | solution.py:17
Sparse Core Ops, SparseCore 0:
  46.4 75.3 all-reduce.1
